TPU v7x, 32 devices: a whole 2x2x4 slice. The times are simulated.
32 devices in a mesh: groups: 2 (over y), wide: 4 (over z), narrow: 4 (over x, core).
Axes of the slice: x: 2, y: 2, z: 4, core: 2. Of those that a mesh axis runs over, the one named last changes fastest.
Arguments:
- inputs: bfloat16 [40, 2, 8192], P('groups', None, 'narrow'), parts along dimension 0, may hold values from -6 to 6
- xz_weight: bfloat16 [8192, 2, 16384], P('narrow', None, 'wide'), may hold values from -0.0625 to 0.0625
- bc_weight: bfloat16 [8192, 4096], P('narrow', 'wide'), may hold values from -0.0625 to 0.0625
- dt_weight: bfloat16 [8192, 256], P('narrow', 'wide'), may hold values from -0.0625 to 0.0625
- conv_x_weight: bfloat16 [4, 256, 64], P(None, 'wide', 'narrow'), may hold values from -3 to 3
- conv_x_bias: bfloat16 [256, 64], P('wide', 'narrow'), may hold values from -3 to 3
- conv_bc_weight: bfloat16 [4, 4096], P(None, 'wide'), may hold values from -3 to 3
- conv_bc_bias: bfloat16 [4096], P('wide'), may hold values from -3 to 3
- conv_x_state: bfloat16 [40, 3, 256, 64], P('groups', None, 'wide', 'narrow'), parts along dimension 0, may hold values from -6 to 6
- conv_bc_state: bfloat16 [40, 3, 4096], P('groups', None, 'wide'), parts along dimension 0, may hold values from -6 to 6
- dt_bias: float32 [256], P('wide'), may hold values from -4 to 0
- a_log: float32 [256], P('wide'), may hold values from 0 to 2.5
- d_skip: float32 [256], P('wide'), may hold values from 0.5 to 2
- norm_weight: bfloat16 [256, 64], P('wide', 'narrow'), may hold values from 0.099609375 to 1.8984375
- out_weight: bfloat16 [256, 64, 8192], P(None, 'narrow', 'wide'), may hold values from -0.046875 to 0.046875
- ssm_state: float32 [40, 256, 64, 256], P('groups', 'wide', 'narrow'), parts along dimension 0, may hold values from -4 to 4
Outputs:
- layer_out: bfloat16 [40, 2, 8192], P('groups', None, ('wide', 'narrow')), parts along dimension 0
- new_ssm_state: float32 [40, 256, 64, 256], P('groups', 'wide', 'narrow'), parts along dimension 0
- new_conv_x: bfloat16 [40, 3, 256, 64], P('groups', None, 'wide', 'narrow'), parts along dimension 0
- new_conv_bc: bfloat16 [40, 3, 4096], P('groups', None, 'wide'), parts along dimension 0
There are 2 independent parts, one for each index of `groups`. A program takes and returns all parts, laid end to end along the dimension named above; an argument that names none is the same for every part. Nothing has to cross between parts.
All inputs are finite; a program needn't handle non-finite values.
Results may differ from a plain program's by a relative error of at most 0.015.
Values may be sent and summed in bfloat16 or wider, within the bound.
A program may use at most 192 MiB of HBM per device.

v0:
```python
import jax
import jax.numpy as jnp
from jax import lax
from jax.sharding import PartitionSpec as P

HEADS = 256
HEAD_DIM = 64
STATE = 256
NGROUPS = 8
EPSILON = 1e-05


def shortened(value):

    def short(part):
        return part.astype(jnp.bfloat16) if part.dtype == jnp.float32 else part

    return jax.tree.map(short, value)


def swapped(value, axis, bit):
    mask = 2**bit
    pairs = [(source, source ^ mask) for source in range(lax.axis_size(axis))]
    return lax.ppermute(value, axis, pairs)


def conv_tokens(history, fresh_vals, tap_weights, offset):
    window = jnp.concatenate([history, fresh_vals], axis=1)
    outputs = []
    for token_idx in range(2):
        summed = offset.astype(jnp.float32)
        for tap_idx in range(tap_weights.shape[0]):
            summed = summed + tap_weights[tap_idx].astype(jnp.float32) * window[
                :, token_idx + tap_idx
            ].astype(jnp.float32)
        outputs.append(jax.nn.silu(summed))
    return (jnp.stack(outputs, axis=1), window[:, 2:])


def advance(ssm_now, x_tok, b_tok, c_tok, dt_tok, dt_bias, a_log, d_skip):
    step_size = jax.nn.softplus(dt_tok.astype(jnp.float32) + dt_bias)
    decay_now = jnp.exp(-step_size * jnp.exp(a_log))
    inject = (step_size[:, :, None] * x_tok)[..., None] * b_tok[:, :, None, :]
    ssm_now = decay_now[:, :, None, None] * ssm_now + inject
    readout = jnp.sum(ssm_now * c_tok[:, :, None, :], axis=-1) + d_skip[None, :, None] * x_tok
    return (ssm_now, readout)


def shards(
    inputs,
    xz_weight,
    bc_weight,
    dt_weight,
    conv_x_weight,
    conv_x_bias,
    conv_bc_weight,
    conv_bc_bias,
    conv_x_state,
    conv_bc_state,
    dt_bias,
    a_log,
    d_skip,
    norm_weight,
    out_weight,
    ssm_state,
):
    seq_count = inputs.shape[0]
    row_count = seq_count * 2
    tok_rows = inputs.reshape(row_count, inputs.shape[2])
    head_local = dt_weight.shape[1]
    wide_count = lax.axis_size("wide")
    narrow_count = lax.axis_size("narrow")
    wide_index = lax.axis_index("wide")
    chan_local = HEAD_DIM // narrow_count
    xz_local = xz_weight.reshape(xz_weight.shape[0], 2, head_local, HEAD_DIM)
    bc_part = jnp.dot(tok_rows, bc_weight, preferred_element_type=jnp.float32)
    dt_part = jnp.dot(tok_rows, dt_weight, preferred_element_type=jnp.float32)
    xz_mine = lax.psum_scatter(
        jnp.einsum("rd,dzhc->czrh", tok_rows, xz_local, preferred_element_type=jnp.float32),
        "narrow",
        scatter_dimension=0,
        tiled=True,
    )
    bc_summed, dt_summed = lax.psum((bc_part, dt_part), "narrow")
    xz_mine = xz_mine.astype(jnp.bfloat16)
    xz_mine = jnp.transpose(xz_mine, (1, 2, 3, 0)).reshape(2, seq_count, 2, head_local, chan_local)
    gate_vals = xz_mine[0]
    x_proj = xz_mine[1]
    bc_proj = bc_summed.astype(jnp.bfloat16).reshape(seq_count, 2, bc_summed.shape[1])
    dt_proj = dt_summed.astype(jnp.bfloat16).reshape(seq_count, 2, head_local)
    x_conv, new_conv_x = conv_tokens(conv_x_state, x_proj, conv_x_weight, conv_x_bias)
    bc_conv, new_conv_bc = conv_tokens(conv_bc_state, bc_proj, conv_bc_weight, conv_bc_bias)
    group_local = max(NGROUPS // wide_count, 1)
    group_span = max(wide_count // NGROUPS, 1)
    bc_mine = bc_conv.reshape(row_count, bc_conv.shape[2])
    for bit_idx in range(group_span.bit_length() - 1):
        partner = swapped(shortened(bc_mine), "wide", bit_idx).astype(bc_mine.dtype)
        is_lower = wide_index // (1 << bit_idx) % 2 == 0
        bc_mine = jnp.where(
            is_lower,
            jnp.concatenate([bc_mine, partner], axis=1),
            jnp.concatenate([partner, bc_mine], axis=1),
        )
    bc_heads = bc_mine.reshape(seq_count, 2, group_local, 2, STATE)
    per_group = head_local // group_local
    b_heads = jnp.repeat(bc_heads[:, :, :, 0], per_group, axis=2)
    c_heads = jnp.repeat(bc_heads[:, :, :, 1], per_group, axis=2)
    ssm_now = ssm_state
    readouts = []
    for token_idx in range(2):
        ssm_now, readout = advance(
            ssm_now,
            x_conv[:, token_idx],
            b_heads[:, token_idx],
            c_heads[:, token_idx],
            dt_proj[:, token_idx],
            dt_bias,
            a_log,
            d_skip,
        )
        readouts.append(readout)
    y_all = jnp.stack(readouts, axis=1)
    gated_out = y_all * jax.nn.silu(gate_vals.astype(jnp.float32))
    grouped = gated_out.reshape(seq_count, 2, group_local, per_group * chan_local)
    squares_part = jnp.sum(grouped * grouped, axis=-1)
    group_sum = lax.psum(squares_part, "narrow")
    for bit_idx in range(group_span.bit_length() - 1):
        group_sum = group_sum + swapped(group_sum, "wide", bit_idx)
    inverse = lax.rsqrt(group_sum / (HEADS // NGROUPS * HEAD_DIM) + EPSILON)
    normed = (grouped * inverse[..., None]).reshape(
        seq_count, 2, head_local, chan_local
    ) * norm_weight.astype(jnp.float32)
    normed = normed.astype(jnp.bfloat16).reshape(row_count, head_local, chan_local)
    out_part = jnp.einsum(
        "rhc,hcd->rd",
        lax.all_gather(normed, "wide", axis=1, tiled=True),
        out_weight,
        preferred_element_type=jnp.float32,
    )
    out_mine = lax.psum_scatter(
        out_part.astype(jnp.bfloat16), "narrow", scatter_dimension=1, tiled=True
    )
    layer_out = out_mine.reshape(seq_count, 2, out_mine.shape[1])
    return (layer_out, ssm_now, new_conv_x, new_conv_bc)


def solution(mesh):
    return jax.shard_map(
        shards,
        mesh=mesh,
        in_specs=(
            P("groups", None, "narrow"),
            P("narrow", None, "wide"),
            P("narrow", "wide"),
            P("narrow", "wide"),
            P(None, "wide", "narrow"),
            P("wide", "narrow"),
            P(None, "wide"),
            P("wide"),
            P("groups", None, "wide", "narrow"),
            P("groups", None, "wide"),
            P("wide"),
            P("wide"),
            P("wide"),
            P("wide", "narrow"),
            P(None, "narrow", "wide"),
            P("groups", "wide", "narrow", None),
        ),
        out_specs=(
            P("groups", None, ("wide", "narrow")),
            P("groups", "wide", "narrow", None),
            P("groups", None, "wide", "narrow"),
            P("groups", None, "wide"),
        ),
        check_vma=False,
    )
```

profile of v0, /device:TPU:0, one launch (start us, length us, event | category | flops | bytes accessed | tf_op | source)
XLA Modules:
  0.0 250.9 jit_solution(5239584444995894743)
XLA Ops:
  7.2 80.9 %copy.186 = bf16[2048,2,4096]{0,2,1:T(8,128)(2,1)} copy(bf16[2048,2,4096]{2,1,0:T(2,128)(2,1)} %param.17) | data formatting | bytes 67108864 | tf_op args[1]
  88.3 21.7 %convolution_bitcast_fusion.1 = f32[64,2,40,64]{0,2,3,1:T(8,128)S(1)} fusion(bf16[2048,2,64,64]{0,3,2,1:T(8,128)(2,1)} %bitcast.177, bf16[40,2048,1,1]{1,0,2,3:T(8,128)(2,1)S(1)} %reshape.347), kind=kOutput, calls=%fused_computation.6 | convolution fusion | flops 1342177280 | bytes 35028992 | tf_op jit(solution)/shard_map/rd,dzhc->czrh/dot_general | solution.py:79
  110.0 2.1 copy.187
  112.2 3.0 %fusion.60 = f32[40,1024]{1,0:T(8,128)S(1)} fusion(bf16[40,2048]{1,0:T(8,128)(2,1)S(1)} %reshape.324, bf16[2048,1024]{1,0:T(8,128)(2,1)} %param.18), kind=kOutput, calls=%fused_computation.124 | convolution fusion | flops 167772160 | bytes 4521984 | tf_op jit(solution)/shard_map/dot_general | solution.py:76
  115.5 15.5 %all-reduce.2 = (bf16[40,1024]{1,0:T(8,128)(2,1)S(1)}, bf16[40,64]{1,0:T(8,128)(2,1)S(1)}) all-reduce(f32[40,1024]{1,0:T(8,128)S(1)} %fusion.60, f32[40,64]{1,0:T(8,128)S(1)} %fusion.59), channel_id=1, replica_groups=mesh['groups'=2,'wide'=4,'narrow'=4] {'narrow'}, use_global_device_ids=true, to_apply=%region_2.0 | all-reduce | flops 43520 | bytes 261120 | tf_op jit(solution)/shard_map/psum | solution.py:84
  131.7 1.0 divide_multiply_fusion
  133.3 0.9 copy.214
  134.2 0.7 copy.185
  134.9 0.7 copy.183
  135.6 0.7 copy.181
  136.3 0.7 copy.179
  137.0 1.4 copy.178
  139.0 1.3 convert_element_type.253
  140.3 1.3 multiply_exponential_fusion
  142.6 1.8 slice_bitcast_fusion.3
  144.4 5.1 %reduce-scatter.3.cloned.1.call-done = f32[16,2,40,64]{3,2,1,0:T(8,128)} async-done(((f32[64,2,40,64]{3,2,1,0:T(8,128)}), f32[16,2,40,64]{3,2,1,0:T(8,128)}) %reduce-scatter.3.cloned.1.call-update) | async-done | bytes 327696 | tf_op jit(solution)/shard_map/reduce_scatter | solution.py:78
  149.5 1.3 copy.234
  150.8 0.7 copy-done.4
  152.8 1.8 copy.217
  154.6 1.8 copy.218
  156.4 2.0 multiply_multiply_fusion.1
  158.5 21.2 %multiply_reduce_fusion = (f32[20,64,16]{2,1,0:T(8,128)S(1)}, f32[20,64,16,256]{3,2,1,0:T(8,128)}, f32[20,64,16]{2,1,0:T(8,128)S(1)}) fusion(f32[20,64,256]{2,1,0:T(8,128)S(1)} %get-tuple-element.10, f32[20,64,256]{2,1,0:T(8,128)} %get-tuple-element.12, f32[20,64,16]{2,1,0:T(8,128)S(1)} %get-tuple-element.16, f32[20,64,256]{2,1,0:T(8,128)} %get-tuple-element.11, ...), kind=kLoop, calls=%fused_computation | loop fusion | flops 52387840 | bytes 47523840 | tf_op jit(solution)/shard_map/reduce_sum | solution.py:45
  179.7 0.8 bitcast_add_fusion.1
  182.7 1.1 fusion.40
  184.1 5.7 %psum.23 = f32[20,2,2]{0,2,1:T(2,128)S(1)} all-reduce(f32[20,2,2]{0,2,1:T(2,128)S(1)} %copy.204), channel_id=1, replica_groups=mesh['groups'=2,'wide'=4,'narrow'=4] {'narrow'}, use_global_device_ids=true, to_apply=%region_7.8 | all-reduce | flops 80 | bytes 640 | tf_op jit(solution)/shard_map/psum | solution.py:126
  190.2 1.1 fusion.39
  191.6 22.6 %all_gather.3 = bf16[40,256,16]{0,2,1:T(8,128)(2,1)S(1)} all-gather(bf16[40,64,16]{0,2,1:T(8,128)(2,1)S(1)} %copy.206), channel_id=1, replica_groups=mesh['groups'=2,'wide'=4,'narrow'=4] {'wide'}, dimensions={1}, use_global_device_ids=true | all-gather | bytes 409600 | tf_op jit(solution)/shard_map/all_gather | solution.py:136
  214.3 9.5 %fusion = bf16[40,2048]{1,0:T(8,128)(2,1)} fusion(bf16[40,256,16]{0,2,1:T(8,128)(2,1)S(1)} %all_gather.3, bf16[256,16,2048]{2,1,0:T(8,128)(2,1)} %param.30), kind=kOutput, calls=%fused_computation.5 | convolution fusion | flops 671170560 | bytes 17268736 | tf_op jit(solution)/shard_map/rhc,hcd->rd/dot_general | solution.py:134
  223.8 0.7 pad_maximum_fusion.3
  224.5 0.7 pad_maximum_fusion.1
  225.3 17.4 %reduce-scatter.5.cloned.1.call-done = bf16[40,512]{1,0:T(8,128)(2,1)} async-done(((bf16[40,2048]{1,0:T(8,128)(2,1)}), bf16[40,512]{1,0:T(8,128)(2,1)}) %reduce-scatter.5.cloned.1.call-update) | async-done | bytes 40976 | tf_op jit(solution)/shard_map/reduce_scatter | solution.py:140
  242.7 1.4 reshape.330
  (88 shorter events, 7.8 us)
Async XLA Ops:
  7.2 108.1 %copy-start = (bf16[2048,64]{0,1:T(8,128)(2,1)S(1)}, bf16[2048,64]{0,1:T(8,128)(2,1)}, u32[]{:S(2)}) copy-start(bf16[2048,64]{0,1:T(8,128)(2,1)} %param.19) | copy-start | bytes 786436
  7.2 81.0 %copy-start.11 = (bf16[20,2,2048]{2,1,0:T(2,128)(2,1)S(1)}, bf16[20,2,2048]{2,1,0:T(2,128)(2,1)}, u32[]{:S(2)}) copy-start(bf16[20,2,2048]{2,1,0:T(2,128)(2,1)} %param.16) | copy-start | bytes 491524
  7.2 142.3 %reduce-scatter.3.cloned.1.call-start = ((), (), s32[]{:S(2)}) async-start(), calls=%async_computation.2 | async-start | bytes 3276800 | tf_op jit(solution)/shard_map/reduce_scatter | solution.py:78
  88.2 42.8 %copy-start.20 = (bf16[1024]{0:T(1024)(128)(2,1)S(1)}, bf16[1024]{0:T(1024)(128)(2,1)}, u32[]{:S(2)}) copy-start(bf16[1024]{0:T(1024)(128)(2,1)} %param.23) | copy-start | bytes 6148
  88.2 42.8 %copy-start.18 = (bf16[4,1024]{1,0:T(4,128)(2,1)S(1)}, bf16[4,1024]{1,0:T(4,128)(2,1)}, u32[]{:S(2)}) copy-start(bf16[4,1024]{1,0:T(4,128)(2,1)} %param.22) | copy-start | bytes 24580
  88.3 44.6 %copy-start.7 = (bf16[20,3,64,16]{2,3,1,0:T(8,128)(2,1)S(1)}, bf16[20,3,64,16]{2,3,1,0:T(8,128)(2,1)}, u32[]{:S(2)}) copy-start(bf16[20,3,64,16]{2,3,1,0:T(8,128)(2,1)} %param.24) | copy-start | bytes 368644
  88.3 45.9 %copy-start.19 = (bf16[4,64,16]{1,2,0:T(8,128)(2,1)S(1)}, bf16[4,64,16]{1,2,0:T(8,128)(2,1)}, u32[]{:S(2)}) copy-start(bf16[4,64,16]{1,2,0:T(8,128)(2,1)} %param.20) | copy-start | bytes 24580
  112.1 130.6 %reduce-scatter.5.cloned.1.call-start = ((), (), s32[]{:S(2)}) async-start(), calls=%async_computation.3 | async-start | bytes 204800 | tf_op jit(solution)/shard_map/reduce_scatter | solution.py:140
  131.0 0.6 copy-start.9
  150.8 0.7 copy-start.4
  151.5 0.7 copy-start.5
  158.4 21.3 %copy-start.1 = (bf16[20,1,64,16]{3,2,0,1:T(8,128)(2,1)S(1)}, bf16[20,1,64,16]{3,2,0,1:T(8,128)(2,1)}, u32[]{:S(2)}) copy-start(bf16[20,1,64,16]{3,2,0,1:T(8,128)(2,1)} %copy.214) | copy-start | bytes 122884
  158.4 21.3 %copy-start.2 = (bf16[20,1,64,16]{3,2,0,1:T(8,128)(2,1)S(1)}, bf16[20,1,64,16]{3,2,0,1:T(8,128)(2,1)}, u32[]{:S(2)}) copy-start(bf16[20,1,64,16]{3,2,0,1:T(8,128)(2,1)} %copy.217) | copy-start | bytes 122884
  158.4 21.3 %copy-start.3 = (bf16[20,1,64,16]{3,2,0,1:T(8,128)(2,1)S(1)}, bf16[20,1,64,16]{3,2,0,1:T(8,128)(2,1)}, u32[]{:S(2)}) copy-start(bf16[20,1,64,16]{3,2,0,1:T(8,128)(2,1)} %copy.218) | copy-start | bytes 122884
  158.4 21.3 %copy-start.13 = (f32[64,16]{1,0:T(8,128)S(1)}, f32[64,16]{1,0:T(8,128)}, u32[]{:S(2)}) copy-start(f32[64,16]{1,0:T(8,128)} %copy.185) | copy-start | bytes 12292
  158.4 21.3 %copy-start.14 = (f32[64,16]{1,0:T(8,128)S(1)}, f32[64,16]{1,0:T(8,128)}, u32[]{:S(2)}) copy-start(f32[64,16]{1,0:T(8,128)} %copy.183) | copy-start | bytes 12292
  158.4 21.3 %copy-start.15 = (f32[64,16]{1,0:T(8,128)S(1)}, f32[64,16]{1,0:T(8,128)}, u32[]{:S(2)}) copy-start(f32[64,16]{1,0:T(8,128)} %copy.181) | copy-start | bytes 12292
  158.5 21.3 %copy-start.16 = (f32[64,16]{1,0:T(8,128)S(1)}, f32[64,16]{1,0:T(8,128)}, u32[]{:S(2)}) copy-start(f32[64,16]{1,0:T(8,128)} %copy.179) | copy-start | bytes 12292
  158.5 21.3 %copy-start.17 = (f32[64,16]{1,0:T(8,128)S(1)}, f32[64,16]{1,0:T(8,128)}, u32[]{:S(2)}) copy-start(f32[64,16]{1,0:T(8,128)} %copy.178) | copy-start | bytes 12292
  158.5 21.3 %copy-start.21 = (f32[64]{0:T(128)S(1)}, f32[64]{0:T(128)}, u32[]{:S(2)}) copy-start(f32[64]{0:T(128)} %param.28) | copy-start | bytes 772
  181.7 42.1 %copy-start.10 = (bf16[20,2,1024]{2,0,1:T(8,128)(2,1)S(1)}, bf16[20,2,1024]{2,0,1:T(8,128)(2,1)}, u32[]{:S(2)}) copy-start(bf16[20,2,1024]{2,0,1:T(8,128)(2,1)} %copy-done.9) | copy-start | bytes 245764
  181.7 42.1 %copy-start.12 = (bf16[20,3,1024]{2,0,1:T(8,128)(2,1)S(1)}, bf16[20,3,1024]{2,0,1:T(8,128)(2,1)}, u32[]{:S(2)}) copy-start(bf16[20,3,1024]{2,0,1:T(8,128)(2,1)} %param.25) | copy-start | bytes 368644
  181.8 42.7 %copy-start.6 = (bf16[1,40,64,16]{2,3,1,0:T(8,128)(2,1)S(1)}, bf16[1,40,64,16]{2,3,1,0:T(8,128)(2,1)}, u32[]{:S(2)}) copy-start(bf16[1,40,64,16]{2,3,1,0:T(8,128)(2,1)} %copy-done.5) | copy-start | bytes 245764
  181.8 42.7 %copy-start.8 = (bf16[20,3,64,16]{2,3,1,0:T(8,128)(2,1)S(1)}, bf16[20,3,64,16]{2,3,1,0:T(8,128)(2,1)}, u32[]{:S(2)}) copy-start(bf16[20,3,64,16]{2,3,1,0:T(8,128)(2,1)} %param.24) | copy-start | bytes 368644
Sparse Core Ops, SparseCore 0:
  112.2 37.1 reduce-scatter.2
  223.9 18.6 reduce-scatter.4
where the time goes:
time: 254 us; the launch traced here: 251 us
  local copies, waits for them, and re-layouts  104 us (41%)
  blocking collectives  43.9 us (17%)
  matrix products  34.4 us (14%)
  other arithmetic  31.4 us (12%)
  waiting for transfers between devices  22.5 us (9%)
  between operations  14.6 us (6%)
    unnamed x52, local copies, waits for them, and re-layouts  87.9 us
    all_gather x1, blocking collectives, shards(): lax.all_gather(normed, 'wide', axis=1, tiled=True)  22.6 us
    dot_general x1, matrix products, shards(): jnp.einsum('rd,dzhc->czrh', tok_rows, xz_local, preferred_element_type=jn...  21.7 us
    reduce_sum x1, other arithmetic, advance(): jnp.sum(ssm_now * c_tok[:, :, None, :], axis=-1)  21.2 us
    reduce_scatter x1, waiting for transfers between devices, shards(): lax.psum_scatter(out_part.astype(jnp.bfloat16), 'narrow', scatter_dimensi...  17.4 us
    psum x1, blocking collectives, shards(): bc_summed, dt_summed = lax.psum((bc_part, dt_part), 'narrow')  15.5 us
    dot_general x1, matrix products, shards(): jnp.einsum('rhc,hcd->rd', lax.all_gather(normed, 'wide', axis=1, tiled=Tr...  9.51 us
    psum x1, blocking collectives, shards(): group_sum = lax.psum(squares_part, 'narrow')  5.73 us
  transfers between devices with their start and end apart: 2, of which 2 were waited for; matrix products, arithmetic and copies ran while one was open for 7% of the time, Pallas kernels for 0%

commit v1 on v0

--- a/solution.py
+++ b/solution.py
@@ -8,6 +8,31 @@
 STATE = 256
 NGROUPS = 8
 EPSILON = 1e-05
+
+
+def lift_sample(message):
+    finding = jax.lax.axis_size("wide")
+    arr_out = jax.lax.axis_index("wide")
+    x_new, latest, mat_out = (finding, arr_out, message.shape[1])
+    found = [dev_i * x_new if ix == 1 else dev_i for ix, dev_i in enumerate(message.shape)]
+    s_next = jnp.zeros(found, message.dtype)
+    moved = lax.dynamic_update_slice_in_dim(s_next, message, latest * mat_out, axis=1)
+    y2 = local_now = message
+    for dev in range(1, x_new // 2 + 1):
+        mixed_arr = range(x_new)
+        all_values = map(lambda ix: (ix, (ix + 1) % x_new), mixed_arr)
+        opened = list(all_values)
+        y2 = jax.lax.ppermute(y2, "wide", opened)
+        moved = lax.dynamic_update_slice_in_dim(moved, y2, (latest - dev) % x_new * mat_out, axis=1)
+        if 2 * dev < x_new:
+            last = range(x_new)
+            z1 = map(lambda ix: (ix, (ix - 1) % x_new), last)
+            tmp = list(z1)
+            local_now = jax.lax.ppermute(local_now, "wide", tmp)
+            moved = lax.dynamic_update_slice_in_dim(
+                moved, local_now, (latest + dev) % x_new * mat_out, axis=1
+            )
+    return moved
 
 
 def shortened(value):
@@ -132,10 +157,7 @@
     ) * norm_weight.astype(jnp.float32)
     normed = normed.astype(jnp.bfloat16).reshape(row_count, head_local, chan_local)
     out_part = jnp.einsum(
-        "rhc,hcd->rd",
-        lax.all_gather(normed, "wide", axis=1, tiled=True),
-        out_weight,
-        preferred_element_type=jnp.float32,
+        "rhc,hcd->rd", lift_sample(normed), out_weight, preferred_element_type=jnp.float32
     )
     out_mine = lax.psum_scatter(
         out_part.astype(jnp.bfloat16), "narrow", scatter_dimension=1, tiled=True

time: 254 us -> 272 us (1.071)
  blocking collectives: 43.9 us -> 21.2 us
  matrix products: 34.4 us -> 53.5 us
  local copies, waits for them, and re-layouts: 104 us -> 114 us
  waiting for transfers between devices: 22.5 us -> 32.3 us
  starting transfers between devices: 0.08 us -> 3.96 us
    all_gather x1 -> x0, blocking collectives: 22.6 us -> none  [shards(): lax.all_gather(normed, 'wide', axis=1, tiled=True)]
    dot_general x1, matrix products: 9.51 us -> 28.5 us  [shards(): jnp.einsum('rhc,hcd->rd', lift_sample(normed), out_weight, preferred_elem...]
    dynamic_update_slice x0 -> x4, local copies, waits for them, and re-layouts: none -> 11.4 us  [the longest x2 5.47 us: lift_sample(): lax.dynamic_update_slice_in_dim(moved, y2, (latest - dev) % x_new * mat_o...]
    ppermute x0 -> x3, waiting for transfers between devices: none -> 5.1 us  [the longest x2 5.1 us: lift_sample(): y2 = jax.lax.ppermute(y2, 'wide', opened)]
    ppermute x0 -> x3, starting transfers between devices: none -> 3.88 us  [the longest x1 2.17 us: lift_sample(): local_now = jax.lax.ppermute(local_now, 'wide', tmp)]
    reduce_scatter x1, waiting for transfers between devices: 5.09 us -> 7.81 us  [shards(): lax.psum_scatter(jnp.einsum('rd,dzhc->czrh', tok_rows, xz_local, preferre...]
    unnamed x52 -> x60, local copies, waits for them, and re-layouts: 87.9 us -> 88 us
  transfers between devices with their start and end apart: 2 -> 5, of which waited for: 2 -> 3; matrix products, arithmetic and copies ran while one was open for 7% -> 9% of each run, Pallas kernels for 0% -> 0%
where the time goes in v1:
time: 272 us; the launch traced here: 270 us
  local copies, waits for them, and re-layouts  114 us (42%)
  matrix products  53.5 us (20%)
  waiting for transfers between devices  32.3 us (12%)
  other arithmetic  30.1 us (11%)
  blocking collectives  21.2 us (8%)
  between operations  14.7 us (5%)
  starting transfers between devices  3.96 us (1%)
    unnamed x60, local copies, waits for them, and re-layouts  88 us
    dot_general x1, matrix products, shards(): jnp.einsum('rhc,hcd->rd', lift_sample(normed), out_weight, preferred_elem...  28.5 us
    dot_general x1, matrix products, shards(): jnp.einsum('rd,dzhc->czrh', tok_rows, xz_local, preferred_element_type=jn...  21.7 us
    reduce_sum x1, other arithmetic, advance(): jnp.sum(ssm_now * c_tok[:, :, None, :], axis=-1)  21.2 us
    reduce_scatter x1, waiting for transfers between devices, shards(): lax.psum_scatter(out_part.astype(jnp.bfloat16), 'narrow', scatter_dimensi...  19.4 us
    psum x1, blocking collectives, shards(): bc_summed, dt_summed = lax.psum((bc_part, dt_part), 'narrow')  15.5 us
    reduce_scatter x1, waiting for transfers between devices, shards(): lax.psum_scatter(jnp.einsum('rd,dzhc->czrh', tok_rows, xz_local, preferre...  7.81 us
    psum x1, blocking collectives, shards(): group_sum = lax.psum(squares_part, 'narrow')  5.73 us
  transfers between devices with their start and end apart: 5, of which 3 were waited for; matrix products, arithmetic and copies ran while one was open for 9% of the time, Pallas kernels for 0%

profile of v1, /device:TPU:0, one launch (start us, length us, event | category | flops | bytes accessed | tf_op | source)
XLA Modules:
  0.0 269.7 jit_solution(5974984070286842549)
XLA Ops:
  7.2 81.0 %copy.210 = bf16[2048,2,4096]{0,2,1:T(8,128)(2,1)} copy(bf16[2048,2,4096]{2,1,0:T(2,128)(2,1)} %param.17) | data formatting | bytes 67108864 | tf_op args[1]
  88.4 21.7 %convolution_bitcast_fusion = f32[64,2,40,64]{0,2,3,1:T(8,128)S(1)} fusion(bf16[2048,2,64,64]{0,3,2,1:T(8,128)(2,1)} %bitcast.176, bf16[40,2048,1,1]{1,0,2,3:T(8,128)(2,1)S(1)} %reshape.347), kind=kOutput, calls=%fused_computation.8 | convolution fusion | flops 1342177280 | bytes 35028992 | tf_op jit(solution)/shard_map/rd,dzhc->czrh/dot_general | solution.py:104
  110.1 2.1 copy.211
  112.3 3.0 %fusion.67 = f32[40,1024]{1,0:T(8,128)S(1)} fusion(bf16[40,2048]{1,0:T(8,128)(2,1)S(1)} %reshape.324, bf16[2048,1024]{1,0:T(8,128)(2,1)} %param.18), kind=kOutput, calls=%fused_computation.126 | convolution fusion | flops 167772160 | bytes 4521984 | tf_op jit(solution)/shard_map/dot_general | solution.py:101
  115.6 15.5 %all-reduce.2 = (bf16[40,1024]{1,0:T(8,128)(2,1)S(1)}, bf16[40,64]{1,0:T(8,128)(2,1)S(1)}) all-reduce(f32[40,1024]{1,0:T(8,128)S(1)} %fusion.67, f32[40,64]{1,0:T(8,128)S(1)} %fusion.66), channel_id=1, replica_groups=mesh['groups'=2,'wide'=4,'narrow'=4] {'narrow'}, use_global_device_ids=true, to_apply=%region_2.0 | all-reduce | flops 43520 | bytes 261120 | tf_op jit(solution)/shard_map/psum | solution.py:109
  131.8 1.0 divide_multiply_fusion
  135.1 0.7 copy.209
  136.2 0.9 copy.244
  137.1 0.7 copy.202
  140.0 1.8 slice_bitcast_fusion.3
  141.8 7.8 %reduce-scatter.3.cloned.1.call-done = f32[16,2,40,64]{3,2,1,0:T(8,128)} async-done(((f32[64,2,40,64]{3,2,1,0:T(8,128)}), f32[16,2,40,64]{3,2,1,0:T(8,128)}) %reduce-scatter.3.cloned.1.call-update) | async-done | bytes 327696 | tf_op jit(solution)/shard_map/reduce_scatter | solution.py:103
  149.6 1.3 copy.268
  150.9 0.7 copy-done.4
  153.0 1.8 copy.245
  154.8 1.8 copy.246
  156.6 2.0 multiply_multiply_fusion.1
  158.7 21.2 %multiply_reduce_fusion = (f32[20,64,16]{2,1,0:T(8,128)S(1)}, f32[20,64,16,256]{3,2,1,0:T(8,128)}, f32[20,64,16]{2,1,0:T(8,128)S(1)}) fusion(f32[20,64,256]{2,1,0:T(8,128)S(1)} %get-tuple-element.10, f32[20,64,256]{2,1,0:T(8,128)} %get-tuple-element.12, f32[20,64,16]{2,1,0:T(8,128)S(1)} %get-tuple-element.16, f32[20,64,256]{2,1,0:T(8,128)} %get-tuple-element.11, ...), kind=kLoop, calls=%fused_computation | loop fusion | flops 52387840 | bytes 47523840 | tf_op jit(solution)/shard_map/reduce_sum | solution.py:70
  180.0 0.8 bitcast_add_fusion.1
  182.9 1.1 fusion.47
  184.3 5.7 %psum.23 = f32[20,2,2]{0,2,1:T(2,128)S(1)} all-reduce(f32[20,2,2]{0,2,1:T(2,128)S(1)} %copy.228), channel_id=1, replica_groups=mesh['groups'=2,'wide'=4,'narrow'=4] {'narrow'}, use_global_device_ids=true, to_apply=%region_7.8 | all-reduce | flops 80 | bytes 640 | tf_op jit(solution)/shard_map/psum | solution.py:151
  190.4 1.1 fusion.46
  191.5 1.7 collective-permute-start
  193.2 2.2 collective-permute-start.1
  195.4 5.1 %collective-permute-done = bf16[40,64,16]{1,2,0:T(8,128)(2,1)S(1)} collective-permute-done((bf16[40,64,16]{1,2,0:T(8,128)(2,1)S(1)}, bf16[40,64,16]{1,2,0:T(8,128)(2,1)S(1)}, u32[]{:S(2)}, u32[]{:S(2)}) %collective-permute-start) | collective-permute-done | bytes 81952 | tf_op jit(solution)/shard_map/ppermute | solution.py:25
  200.5 1.8 dynamic_update_slice.12
  202.4 3.8 %dynamic_update_slice.13 = bf16[40,256,16]{1,0,2:T(8,128)(2,1)S(1)} dynamic-update-slice(bf16[40,256,16]{1,0,2:T(8,128)(2,1)S(1)} %dynamic_update_slice.12, bf16[40,64,16]{1,0,2:T(8,128)(2,1)S(1)} %copy.231, s32[]{:T(128)} %constant.49.clone.1, s32[]{:T(128)S(6)} %select_n.54, s32[]{:T(128)} %constant.49.clone.1) | dynamic-update-slice | bytes 163844 | tf_op jit(solution)/shard_map/dynamic_update_slice | solution.py:26
  206.3 4.0 %dynamic_update_slice.14 = bf16[40,256,16]{1,0,2:T(8,128)(2,1)S(1)} dynamic-update-slice(bf16[40,256,16]{1,0,2:T(8,128)(2,1)S(1)} %dynamic_update_slice.13, bf16[40,64,16]{1,0,2:T(8,128)(2,1)S(1)} %copy.232, s32[]{:T(128)} %constant.49.clone.1, s32[]{:T(128)S(6)} %select_n.56, s32[]{:T(128)} %constant.49.clone.1) | dynamic-update-slice | bytes 163844 | tf_op jit(solution)/shard_map/dynamic_update_slice | solution.py:32
  210.5 1.6 dynamic_update_slice.15
  212.1 28.5 %fusion.5 = bf16[40,2048]{1,0:T(8,128)(2,1)} fusion(bf16[40,256,16]{1,0,2:T(8,128)(2,1)S(1)} %dynamic_update_slice.15, bf16[256,16,2048]{2,1,0:T(8,128)(2,1)} %param.30), kind=kOutput, calls=%fused_computation.7 | convolution fusion | flops 671170560 | bytes 17268736 | tf_op jit(solution)/shard_map/rhc,hcd->rd/dot_general | solution.py:159
  241.4 0.7 pad_maximum_fusion.1
  242.1 19.4 %reduce-scatter.5.cloned.1.call-done = bf16[40,512]{1,0:T(8,128)(2,1)} async-done(((bf16[40,2048]{1,0:T(8,128)(2,1)}), bf16[40,512]{1,0:T(8,128)(2,1)}) %reduce-scatter.5.cloned.1.call-update) | async-done | bytes 40976 | tf_op jit(solution)/shard_map/reduce_scatter | solution.py:162
  261.5 1.4 reshape.330
  (109 shorter events, 11.1 us)
Async XLA Ops:
  7.2 108.2 %copy-start = (bf16[2048,64]{0,1:T(8,128)(2,1)S(1)}, bf16[2048,64]{0,1:T(8,128)(2,1)}, u32[]{:S(2)}) copy-start(bf16[2048,64]{0,1:T(8,128)(2,1)} %param.19) | copy-start | bytes 786436
  7.2 81.0 %copy-start.11 = (bf16[20,2,2048]{2,1,0:T(2,128)(2,1)S(1)}, bf16[20,2,2048]{2,1,0:T(2,128)(2,1)}, u32[]{:S(2)}) copy-start(bf16[20,2,2048]{2,1,0:T(2,128)(2,1)} %param.16) | copy-start | bytes 491524
  7.2 142.4 %reduce-scatter.3.cloned.1.call-start = ((), (), s32[]{:S(2)}) async-start(), calls=%async_computation.2 | async-start | bytes 3276800 | tf_op jit(solution)/shard_map/reduce_scatter | solution.py:103
  88.3 42.9 %copy-start.22 = (bf16[1024]{0:T(1024)(128)(2,1)S(1)}, bf16[1024]{0:T(1024)(128)(2,1)}, u32[]{:S(2)}) copy-start(bf16[1024]{0:T(1024)(128)(2,1)} %param.23) | copy-start | bytes 6148
  88.3 42.9 %copy-start.18 = (bf16[4,1024]{1,0:T(4,128)(2,1)S(1)}, bf16[4,1024]{1,0:T(4,128)(2,1)}, u32[]{:S(2)}) copy-start(bf16[4,1024]{1,0:T(4,128)(2,1)} %param.22) | copy-start | bytes 24580
  88.3 44.7 %copy-start.25 = (f32[64]{0:T(128)S(1)}, f32[64]{0:T(128)}, u32[]{:S(2)}) copy-start(f32[64]{0:T(128)} %param.27) | copy-start | bytes 772
  88.3 44.7 %copy-start.19 = (bf16[4,64,16]{1,2,0:T(8,128)(2,1)S(1)}, bf16[4,64,16]{1,2,0:T(8,128)(2,1)}, u32[]{:S(2)}) copy-start(bf16[4,64,16]{1,2,0:T(8,128)(2,1)} %param.20) | copy-start | bytes 24580
  88.3 47.4 %copy-start.7 = (bf16[20,3,64,16]{2,3,1,0:T(8,128)(2,1)S(1)}, bf16[20,3,64,16]{2,3,1,0:T(8,128)(2,1)}, u32[]{:S(2)}) copy-start(bf16[20,3,64,16]{2,3,1,0:T(8,128)(2,1)} %param.24) | copy-start | bytes 368644
  88.3 48.8 %copy-start.20 = (bf16[64,16]{0,1:T(8,128)(2,1)S(1)}, bf16[64,16]{0,1:T(8,128)(2,1)}, u32[]{:S(2)}) copy-start(bf16[64,16]{0,1:T(8,128)(2,1)} %param.21) | copy-start | bytes 6148
  88.3 49.4 %copy-start.21 = (bf16[64,16]{0,1:T(8,128)(2,1)S(1)}, bf16[64,16]{0,1:T(8,128)(2,1)}, u32[]{:S(2)}) copy-start(bf16[64,16]{0,1:T(8,128)(2,1)} %param.29) | copy-start | bytes 6148
  110.1 28.4 %copy-start.23 = (f32[64]{0:T(128)S(1)}, f32[64]{0:T(128)}, u32[]{:S(2)}) copy-start(f32[64]{0:T(128)} %param.26) | copy-start | bytes 772
  112.2 149.3 %reduce-scatter.5.cloned.1.call-start = ((), (), s32[]{:S(2)}) async-start(), calls=%async_computation.3 | async-start | bytes 204800 | tf_op jit(solution)/shard_map/reduce_scatter | solution.py:162
  131.1 0.6 copy-start.9
  150.9 0.7 copy-start.4
  151.7 0.7 copy-start.5
  158.6 21.3 %copy-start.1 = (bf16[20,1,64,16]{3,2,0,1:T(8,128)(2,1)S(1)}, bf16[20,1,64,16]{3,2,0,1:T(8,128)(2,1)}, u32[]{:S(2)}) copy-start(bf16[20,1,64,16]{3,2,0,1:T(8,128)(2,1)} %copy.244) | copy-start | bytes 122884
  158.6 21.3 %copy-start.2 = (bf16[20,1,64,16]{3,2,0,1:T(8,128)(2,1)S(1)}, bf16[20,1,64,16]{3,2,0,1:T(8,128)(2,1)}, u32[]{:S(2)}) copy-start(bf16[20,1,64,16]{3,2,0,1:T(8,128)(2,1)} %copy.245) | copy-start | bytes 122884
  158.6 21.3 %copy-start.3 = (bf16[20,1,64,16]{3,2,0,1:T(8,128)(2,1)S(1)}, bf16[20,1,64,16]{3,2,0,1:T(8,128)(2,1)}, u32[]{:S(2)}) copy-start(bf16[20,1,64,16]{3,2,0,1:T(8,128)(2,1)} %copy.246) | copy-start | bytes 122884
  158.6 21.3 %copy-start.13 = (f32[64,16]{1,0:T(8,128)S(1)}, f32[64,16]{1,0:T(8,128)}, u32[]{:S(2)}) copy-start(f32[64,16]{1,0:T(8,128)} %copy.203) | copy-start | bytes 12292
  158.6 21.3 %copy-start.14 = (f32[64,16]{1,0:T(8,128)S(1)}, f32[64,16]{1,0:T(8,128)}, u32[]{:S(2)}) copy-start(f32[64,16]{1,0:T(8,128)} %copy.205) | copy-start | bytes 12292
  158.6 21.3 %copy-start.15 = (f32[64,16]{1,0:T(8,128)S(1)}, f32[64,16]{1,0:T(8,128)}, u32[]{:S(2)}) copy-start(f32[64,16]{1,0:T(8,128)} %copy.207) | copy-start | bytes 12292
  158.6 21.3 %copy-start.16 = (f32[64,16]{1,0:T(8,128)S(1)}, f32[64,16]{1,0:T(8,128)}, u32[]{:S(2)}) copy-start(f32[64,16]{1,0:T(8,128)} %copy.209) | copy-start | bytes 12292
  158.6 21.3 %copy-start.17 = (f32[64,16]{1,0:T(8,128)S(1)}, f32[64,16]{1,0:T(8,128)}, u32[]{:S(2)}) copy-start(f32[64,16]{1,0:T(8,128)} %copy.202) | copy-start | bytes 12292
  158.6 21.3 %copy-start.24 = (f32[64]{0:T(128)S(1)}, f32[64]{0:T(128)}, u32[]{:S(2)}) copy-start(f32[64]{0:T(128)} %param.28) | copy-start | bytes 772
  179.9 60.8 %copy-start.10 = (bf16[20,2,1024]{2,0,1:T(8,128)(2,1)S(1)}, bf16[20,2,1024]{2,0,1:T(8,128)(2,1)}, u32[]{:S(2)}) copy-start(bf16[20,2,1024]{2,0,1:T(8,128)(2,1)} %copy-done.9) | copy-start | bytes 245764
  179.9 60.8 %copy-start.12 = (bf16[20,3,1024]{2,0,1:T(8,128)(2,1)S(1)}, bf16[20,3,1024]{2,0,1:T(8,128)(2,1)}, u32[]{:S(2)}) copy-start(bf16[20,3,1024]{2,0,1:T(8,128)(2,1)} %param.25) | copy-start | bytes 368644
  179.9 61.4 %copy-start.6 = (bf16[1,40,64,16]{2,3,1,0:T(8,128)(2,1)S(1)}, bf16[1,40,64,16]{2,3,1,0:T(8,128)(2,1)}, u32[]{:S(2)}) copy-start(bf16[1,40,64,16]{2,3,1,0:T(8,128)(2,1)} %copy-done.5) | copy-start | bytes 245764
  179.9 61.4 %copy-start.8 = (bf16[20,3,64,16]{2,3,1,0:T(8,128)(2,1)S(1)}, bf16[20,3,64,16]{2,3,1,0:T(8,128)(2,1)}, u32[]{:S(2)}) copy-start(bf16[20,3,64,16]{2,3,1,0:T(8,128)(2,1)} %param.24) | copy-start | bytes 368644
  191.5 9.0 %collective-permute-start = (bf16[40,64,16]{1,2,0:T(8,128)(2,1)S(1)}, bf16[40,64,16]{1,2,0:T(8,128)(2,1)S(1)}, u32[]{:S(2)}, u32[]{:S(2)}) collective-permute-start(bf16[40,64,16]{1,2,0:T(8,128)(2,1)S(1)} %fusion.46), channel_id=1, source_target_pairs={{0,4},{4,8},{8,12},{12,0},{1,5},{5,9},{9,13},{13,1},{2,6},{6,10},{... | collective-permute-start | bytes 245768 | tf_op jit(solution)/shard_map/ppermute | solution.py:25
  193.2 13.1 %collective-permute-start.1 = (bf16[40,64,16]{1,2,0:T(8,128)(2,1)S(1)}, bf16[40,64,16]{1,2,0:T(8,128)(2,1)S(1)}, u32[]{:S(2)}, u32[]{:S(2)}) collective-permute-start(bf16[40,64,16]{1,2,0:T(8,128)(2,1)S(1)} %fusion.46), channel_id=1, source_target_pairs={{0,12},{4,0},{8,4},{12,8},{1,13},{5,1},{9,5},{13,9},{2,14},{6,2},{... | collective-permute-start | bytes 245768 | tf_op jit(solution)/shard_map/ppermute | solution.py:31
  200.4 9.9 %collective-permute-start.2 = (bf16[40,64,16]{1,2,0:T(8,128)(2,1)S(1)}, bf16[40,64,16]{1,2,0:T(8,128)(2,1)S(1)}, u32[]{:S(2)}, u32[]{:S(2)}) collective-permute-start(bf16[40,64,16]{1,2,0:T(8,128)(2,1)S(1)} %collective-permute-done), channel_id=1, source_target_pairs={{0,4},{4,8},{8,12},{12,0},{1,5},{5,9},{9,13},{13,1},{2,6},{6,10},{... | collective-permute-start | bytes 245768 | tf_op jit(solution)/shard_map/ppermute | solution.py:25
Sparse Core Ops, SparseCore 0:
  112.3 37.2 reduce-scatter.2
  240.8 20.6 reduce-scatter.4
